TPU v7x, 256 devices: a whole 4x4x8 slice. The times are simulated.
256 devices in a mesh: dp: 4 (over y), fsdp: 8 (over z), tensor: 8 (over x, core).
Axes of the slice: x: 4, y: 4, z: 8, core: 2. Of those that a mesh axis runs over, the one named last changes fastest.
Arguments:
- momentum: bfloat16 [4, 8192, 8192], P('dp', 'fsdp', 'tensor'), may hold values from -24 to 24
- gradient: bfloat16 [4, 8192, 8192], P('dp', 'fsdp', 'tensor'), may hold values from -4 to 4
- factor: float32 [8192, 256], P('tensor'), may hold values from -6 to 6
Outputs:
- new_momentum: float32 [4, 8192, 8192], P('dp', 'fsdp', 'tensor')
- step_direction: bfloat16 [8192, 8192], P('fsdp', 'tensor')
- new_factor: float32 [8192, 256], P('tensor')
All inputs are finite; a program needn't handle non-finite values.
Results may differ from a plain program's by a relative error of at most 0.0065.
Values may be sent and summed in bfloat16 or wider, within the bound.
A program may use at most 64 MiB of HBM per device.

v0:
```python
import jax
import jax.numpy as jnp
from jax import lax
from jax.sharding import PartitionSpec as P

ROWS = 8192
COLS = 8192
RANK = 256


def orthonormal(rows_part, gram):
    lower = jnp.linalg.cholesky(gram)
    return jax.scipy.linalg.solve_triangular(lower, rows_part.T, lower=True).T


def transposed_product(block, ortho_low):
    return lax.dot_general(
        block, ortho_low, (((0,), (0,)), ((), ())), preferred_element_type=jnp.float32
    )


def local(momentum, gradient, factor):
    highest = lax.Precision.HIGHEST
    replicas = lax.axis_size("dp")
    moment = momentum[0]
    change = gradient[0]
    factor_low = factor.astype(jnp.bfloat16)
    partial_left = jnp.dot(moment, factor_low, preferred_element_type=jnp.float32)
    partial_left = partial_left + jnp.dot(change, factor_low, preferred_element_type=jnp.float32)
    left = lax.psum(partial_left, ("dp", "tensor")) / replicas
    gram = lax.psum(jnp.dot(left.T, left, precision=highest), "fsdp")
    ortho_low = orthonormal(left, gram).astype(jnp.bfloat16)
    partial_right = transposed_product(moment, ortho_low) + transposed_product(change, ortho_low)
    right = lax.psum(partial_right, ("dp", "fsdp")) / replicas
    square_sums = lax.psum(jnp.sum(right * right, axis=0), "tensor")
    new_factor = right / jnp.sqrt(square_sums / COLS + 1e-06)
    right_low = right.astype(jnp.bfloat16)
    feedback = jnp.dot(ortho_low, right_low.T, preferred_element_type=jnp.float32)
    new_momentum = (moment.astype(jnp.float32) + change.astype(jnp.float32) - 0.05 * feedback)[None]
    step_scale = jnp.sqrt(jnp.float32(ROWS / RANK))
    factor_next_low = new_factor.astype(jnp.bfloat16)
    step_direction = (
        step_scale * jnp.dot(ortho_low, factor_next_low.T, preferred_element_type=jnp.float32)
    ).astype(jnp.bfloat16)
    return (new_momentum, step_direction, new_factor)


def solution(mesh):
    in_specs = (P("dp", "fsdp", "tensor"), P("dp", "fsdp", "tensor"), P("tensor", None))
    out_specs = (P("dp", "fsdp", "tensor"), P("fsdp", "tensor"), P("tensor", None))
    return jax.shard_map(local, mesh=mesh, in_specs=in_specs, out_specs=out_specs, check_vma=False)
```

profile of v0, /device:TPU:1, one launch (start us, length us, event | category | flops | bytes accessed | tf_op | source)
XLA Modules:
  0.0 455.1 jit_solution(12589717732364756060)
XLA Ops:
  7.2 0.0 copy-start.1
  7.2 0.0 all-reduce.5.cloned.1.call-start
  7.2 2.7 fusion.2
  10.0 0.0 copy-done.7
  10.0 0.1 copy-done.1
  10.0 1.7 fusion.8
  11.7 0.0 all-reduce.5.cloned.1.call-update
  11.7 0.0 all-reduce.7.cloned.1.call-start
  11.8 119.2 %all-reduce.5.cloned.1.call-done = f32[1024,256]{1,0:T(8,128)} async-done(((f32[1024,256]{1,0:T(8,128)}), f32[1024,256]{1,0:T(8,128)}) %all-reduce.5.cloned.1.call-update) | async-done | bytes 1048592 | tf_op jit(solution)/shard_map/psum | solution.py:30
  131.0 4.2 fusion.17
  135.2 0.0 all-reduce.7.cloned.1.call-update
  135.2 0.2 all-reduce.9.cloned.1.call-start
  135.5 0.1 multiply_bitcast_fusion
  135.5 67.4 %all-reduce.7.cloned.1.call-done = f32[256,256]{0,1:T(8,128)} async-done(((f32[256,256]{0,1:T(8,128)}), f32[256,256]{0,1:T(8,128)}) %all-reduce.7.cloned.1.call-update) | async-done | bytes 262160 | tf_op jit(solution)/shard_map/psum | solution.py:31
  203.0 1.1 copy.7
  204.1 1.0 fusion.24
  205.1 11.7 %cholesky.50 = f32[128,128]{1,0:T(8,128)S(1)} custom-call(f32[128,128]{1,0:T(8,128)S(1)} %cholesky.118), custom_call_target="Cholesky" | custom-call | tf_op jit(solution)/shard_map/jit(cholesky)/cholesky | solution.py:12
  216.8 9.8 %custom-call.15 = f32[1,128,128]{1,2,0:T(8,128)S(1)} custom-call(f32[1,128,128]{2,1,0:T(8,128)S(1)} %get-tuple-element.24), custom_call_target="InvertDiagBlocksLowerTriangular" | custom-call | tf_op jit(solution)/shard_map/jit(cholesky)/cholesky | solution.py:12
  226.7 0.2 constant_dynamic-update-slice_fusion.1
  226.9 0.3 convolution_subtract_fusion.1
  227.1 11.7 %cholesky.105 = f32[128,128]{1,0:T(8,128)S(1)} custom-call(f32[128,128]{1,0:T(8,128)S(1)} %convolution_subtract_fusion.1), custom_call_target="Cholesky" | custom-call | tf_op jit(solution)/shard_map/jit(cholesky)/cholesky | solution.py:12
  238.9 0.6 compare_reduce_fusion
  240.8 0.7 select_select_fusion
  241.6 0.1 triangular_solve.57
  241.6 5.8 %while.1 = (s32[]{:T(128)}, f32[256,256]{1,0:T(8,128)}, s32[2,2]{1,0:T(2,128)S(1)}, f32[2,128,128]{2,1,0:T(8,128)S(1)}, s32[]{:T(128)}) while((s32[]{:T(128)}, f32[256,256]{1,0:T(8,128)}, s32[2,2]{1,0:T(2,128)S(1)}, f32[2,128,128]{2,1,0:T(8,128)S(1)}, s32[]{:T(128)}) %tuple.28), condition=%wide.while_cond, body=%wide.while_body.sunk | while | flops 2 | bytes 131189 | solution.py:13
  241.6 0.6 fusion.40
  242.2 2.3 bitcast_dynamic-update-slice_fusion.2
  244.6 0.6 fusion.40
  245.2 2.3 bitcast_dynamic-update-slice_fusion.2
  247.5 0.0 copy-start
  247.5 19.7 %custom-call.16 = f32[2,128,128]{1,2,0:T(8,128)S(1)} custom-call(f32[2,128,128]{2,1,0:T(8,128)S(1)} %get-tuple-element.10), custom_call_target="InvertDiagBlocksLowerTriangular" | custom-call | tf_op jit(solution)/shard_map/jit(_solve_triangular)/triangular_solve | solution.py:13
  267.2 0.6 fusion.34
  267.8 1.8 convolution_subtract_fusion
  269.7 0.0 copy-start.2
  269.7 0.6 convolution_convert_fusion
  270.3 0.9 fusion
  271.3 1.9 fusion.14
  273.2 0.0 all-reduce.9.cloned.1.call-update
  273.3 149.4 %all-reduce.9.cloned.1.call-done = f32[1024,256]{1,0:T(8,128)} async-done(((f32[1024,256]{1,0:T(8,128)}), f32[1024,256]{1,0:T(8,128)}) %all-reduce.9.cloned.1.call-update) | async-done | bytes 1048592 | tf_op jit(solution)/shard_map/psum | solution.py:34
  422.6 1.4 multiply_reduce_fusion
  424.0 17.3 %psum.31 = f32[256]{0:T(256)S(1)} all-reduce(f32[256]{0:T(256)S(1)} %multiply_reduce_fusion), channel_id=1, replica_groups=mesh['dp'=4,'fsdp'=8,'tensor'=8] {'tensor'}, use_global_device_ids=true, to_apply=%region_8.9 | all-reduce | flops 256 | bytes 2048 | tf_op jit(solution)/shard_map/psum | solution.py:35
  441.3 1.3 multiply_divide_fusion
  442.6 0.0 copy-start.6
  442.6 0.0 copy-start.3
  442.7 2.1 multiply_convert_fusion
  444.8 0.3 copy-done.3
  445.0 0.6 copy-done.4
  445.6 2.9 subtract_bitcast_fusion
  (16 shorter events, 0.1 us)
Async XLA Ops:
  7.2 2.8 copy-start.7
  7.2 2.9 copy-start.1
  7.2 123.8 %all-reduce.5.cloned.1.call-start = ((), (), s32[]{:S(2)}) async-start(), calls=%async_computation | async-start | bytes 2097152 | tf_op jit(solution)/shard_map/psum | solution.py:30
  11.7 191.2 %all-reduce.7.cloned.1.call-start = ((), (), s32[]{:S(2)}) async-start(), calls=%async_computation.1 | async-start | bytes 524288 | tf_op jit(solution)/shard_map/psum | solution.py:31
  131.0 4.4 copy-start.5
  135.2 287.4 %all-reduce.9.cloned.1.call-start = ((), (), s32[]{:S(2)}) async-start(), calls=%async_computation.2 | async-start | bytes 2097152 | tf_op jit(solution)/shard_map/psum | solution.py:34
  247.5 22.9 %copy-start = (bf16[1,1024,1024]{2,1,0:T(8,128)(2,1)S(1)}, bf16[1,1024,1024]{2,1,0:T(8,128)(2,1)}, u32[]{:S(2)}) copy-start(bf16[1,1024,1024]{2,1,0:T(8,128)(2,1)} %param.4) | copy-start | bytes 6291460
  269.7 1.6 copy-start.2
  442.6 6.0 %copy-start.6 = (f32[1024,256]{1,0:T(8,128)}, f32[1024,256]{1,0:T(8,128)S(1)}, u32[]{:S(2)}) copy-start(f32[1024,256]{1,0:T(8,128)S(1)} %multiply_divide_fusion) | copy-start | bytes 3145732
  442.6 2.4 copy-start.3
  442.7 3.0 copy-start.4
Sparse Core Ops, SparseCore 0:
  11.9 119.1 all-reduce.4
  135.3 67.5 all-reduce.6
  273.4 149.1 all-reduce.8
where the time goes:
time: 456 us; the launch traced here: 455 us
  waiting for transfers between devices  336 us (74%)
  other arithmetic  58.1 us (13%)
  matrix products  20.1 us (4%)
  blocking collectives  17.3 us (4%)
  between operations  15.3 us (3%)
  local copies, waits for them, and re-layouts  7.94 us (2%)
    psum x1, waiting for transfers between devices, local(): right = lax.psum(partial_right, ('dp', 'fsdp')) / replicas  149 us
    psum x1, waiting for transfers between devices, local(): left = lax.psum(partial_left, ('dp', 'tensor')) / replicas  119 us
    psum x1, waiting for transfers between devices, local(): gram = lax.psum(jnp.dot(left.T, left, precision=highest), 'fsdp')  67.4 us
    another operation x6, other arithmetic, orthonormal(): lower = jnp.linalg.cholesky(gram)  33.9 us
    another operation x3, other arithmetic, orthonormal(): return jax.scipy.linalg.solve_triangular(lower, rows_part.T, lower=True).T  20.4 us
    psum x1, blocking collectives, local(): square_sums = lax.psum(jnp.sum(right * right, axis=0), 'tensor')  17.3 us
  transfers between devices with their start and end apart: 3, of which 3 were waited for; matrix products, arithmetic and copies ran while one was open for 0% of the time, Pallas kernels for 0%

commit v1 on v0

--- a/solution.py
+++ b/solution.py
@@ -31,7 +31,7 @@
     gram = lax.psum(jnp.dot(left.T, left, precision=highest), "fsdp")
     ortho_low = orthonormal(left, gram).astype(jnp.bfloat16)
     partial_right = transposed_product(moment, ortho_low) + transposed_product(change, ortho_low)
-    right = lax.psum(partial_right, ("dp", "fsdp")) / replicas
+    right = lax.psum(lax.psum(partial_right, "dp"), "fsdp") / replicas
     square_sums = lax.psum(jnp.sum(right * right, axis=0), "tensor")
     new_factor = right / jnp.sqrt(square_sums / COLS + 1e-06)
     right_low = right.astype(jnp.bfloat16)

time: 456 us -> 435 us (0.954)
  waiting for transfers between devices: 336 us -> 316 us
    psum x1 -> x2, waiting for transfers between devices: 149 us -> 130 us  [local(): right = lax.psum(lax.psum(partial_right, 'dp'), 'fsdp') / replicas]
  transfers between devices with their start and end apart: 3 -> 4, of which waited for: 3 -> 4; matrix products, arithmetic and copies ran while one was open for 0% -> 0% of each run, Pallas kernels for 0% -> 0%
where the time goes in v1:
time: 435 us
  waiting for transfers between devices  316 us (73%)
  other arithmetic  58.1 us (13%)
  matrix products  20.1 us (5%)
  blocking collectives  16.9 us (4%)
  between operations  15.3 us (4%)
  local copies, waits for them, and re-layouts  7.94 us (2%)
    psum x2, waiting for transfers between devices, local(): right = lax.psum(lax.psum(partial_right, 'dp'), 'fsdp') / replicas  130 us
    psum x1, waiting for transfers between devices, local(): left = lax.psum(partial_left, ('dp', 'tensor')) / replicas  119 us
    psum x1, waiting for transfers between devices, local(): gram = lax.psum(jnp.dot(left.T, left, precision=highest), 'fsdp')  67.4 us
    another operation x6, other arithmetic, orthonormal(): lower = jnp.linalg.cholesky(gram)  33.9 us
    another operation x3, other arithmetic, orthonormal(): return jax.scipy.linalg.solve_triangular(lower, rows_part.T, lower=True).T  20.4 us
    psum x1, blocking collectives, local(): square_sums = lax.psum(jnp.sum(right * right, axis=0), 'tensor')  16.9 us
  transfers between devices with their start and end apart: 4, of which 4 were waited for; matrix products, arithmetic and copies ran while one was open for 0% of the time, Pallas kernels for 0%

profile of v1, /device:TPU:1, one launch (start us, length us, event | category | flops | bytes accessed | tf_op | source)
XLA Modules:
  0.0 435.1 jit_solution(1810255376577700872)
XLA Ops:
  7.2 0.0 copy-start.1
  7.2 0.0 all-reduce.6.cloned.1.call-start
  7.2 2.7 fusion.2
  10.0 0.1 copy-done.1
  10.0 1.7 fusion.8
  11.7 0.0 all-reduce.6.cloned.1.call-update
  11.7 0.0 all-reduce.8.cloned.1.call-start
  11.8 119.2 %all-reduce.6.cloned.1.call-done = f32[1024,256]{1,0:T(8,128)} async-done(((f32[1024,256]{1,0:T(8,128)}), f32[1024,256]{1,0:T(8,128)}) %all-reduce.6.cloned.1.call-update) | async-done | bytes 1048592 | tf_op jit(solution)/shard_map/psum | solution.py:30
  131.0 4.2 fusion.17
  135.2 0.0 all-reduce.8.cloned.1.call-update
  135.2 0.2 all-reduce.10.cloned.1.call-start
  135.5 0.1 multiply_bitcast_fusion
  135.5 67.4 %all-reduce.8.cloned.1.call-done = f32[256,256]{0,1:T(8,128)} async-done(((f32[256,256]{0,1:T(8,128)}), f32[256,256]{0,1:T(8,128)}) %all-reduce.8.cloned.1.call-update) | async-done | bytes 262160 | tf_op jit(solution)/shard_map/psum | solution.py:31
  203.0 1.1 copy.7
  204.1 1.0 fusion.24
  205.1 11.7 %cholesky.50 = f32[128,128]{1,0:T(8,128)S(1)} custom-call(f32[128,128]{1,0:T(8,128)S(1)} %cholesky.118), custom_call_target="Cholesky" | custom-call | tf_op jit(solution)/shard_map/jit(cholesky)/cholesky | solution.py:12
  216.8 9.8 %custom-call.15 = f32[1,128,128]{1,2,0:T(8,128)S(1)} custom-call(f32[1,128,128]{2,1,0:T(8,128)S(1)} %get-tuple-element.24), custom_call_target="InvertDiagBlocksLowerTriangular" | custom-call | tf_op jit(solution)/shard_map/jit(cholesky)/cholesky | solution.py:12
  226.7 0.2 constant_dynamic-update-slice_fusion.1
  226.9 0.3 convolution_subtract_fusion.1
  227.1 11.7 %cholesky.105 = f32[128,128]{1,0:T(8,128)S(1)} custom-call(f32[128,128]{1,0:T(8,128)S(1)} %convolution_subtract_fusion.1), custom_call_target="Cholesky" | custom-call | tf_op jit(solution)/shard_map/jit(cholesky)/cholesky | solution.py:12
  238.9 0.6 compare_reduce_fusion
  240.8 0.7 select_select_fusion
  241.6 0.1 triangular_solve.57
  241.6 5.8 %while.1 = (s32[]{:T(128)}, f32[256,256]{1,0:T(8,128)}, s32[2,2]{1,0:T(2,128)S(1)}, f32[2,128,128]{2,1,0:T(8,128)S(1)}, s32[]{:T(128)}) while((s32[]{:T(128)}, f32[256,256]{1,0:T(8,128)}, s32[2,2]{1,0:T(2,128)S(1)}, f32[2,128,128]{2,1,0:T(8,128)S(1)}, s32[]{:T(128)}) %tuple.28), condition=%wide.while_cond, body=%wide.while_body.sunk | while | flops 2 | bytes 131189 | solution.py:13
  241.6 0.6 fusion.40
  242.2 2.3 bitcast_dynamic-update-slice_fusion.2
  244.6 0.6 fusion.40
  245.2 2.3 bitcast_dynamic-update-slice_fusion.2
  247.5 0.0 copy-start
  247.5 19.7 %custom-call.16 = f32[2,128,128]{1,2,0:T(8,128)S(1)} custom-call(f32[2,128,128]{2,1,0:T(8,128)S(1)} %get-tuple-element.10), custom_call_target="InvertDiagBlocksLowerTriangular" | custom-call | tf_op jit(solution)/shard_map/jit(_solve_triangular)/triangular_solve | solution.py:13
  267.2 0.6 fusion.34
  267.8 1.8 convolution_subtract_fusion
  269.7 0.6 convolution_convert_fusion
  270.3 0.9 fusion
  271.3 1.9 fusion.14
  273.2 0.0 all-reduce.10.cloned.1.call-update
  273.3 0.0 all-reduce.12.cloned.1.call-start
  273.3 53.1 %all-reduce.10.cloned.1.call-done = f32[1024,256]{1,0:T(8,128)} async-done(((f32[1024,256]{1,0:T(8,128)}), f32[1024,256]{1,0:T(8,128)}) %all-reduce.10.cloned.1.call-update) | async-done | bytes 1048592 | tf_op jit(solution)/shard_map/psum | solution.py:34
  326.4 0.0 all-reduce.12.cloned.1.call-update
  326.4 76.6 %all-reduce.12.cloned.1.call-done = f32[1024,256]{1,0:T(8,128)} async-done(((f32[1024,256]{1,0:T(8,128)}), f32[1024,256]{1,0:T(8,128)}) %all-reduce.12.cloned.1.call-update) | async-done | bytes 1048592 | tf_op jit(solution)/shard_map/psum | solution.py:34
  403.0 1.4 multiply_reduce_fusion
  404.4 16.9 %psum.39 = f32[256]{0:T(256)S(1)} all-reduce(f32[256]{0:T(256)S(1)} %multiply_reduce_fusion), channel_id=1, replica_groups=mesh['dp'=4,'fsdp'=8,'tensor'=8] {'tensor'}, use_global_device_ids=true, to_apply=%region_9.10 | all-reduce | flops 256 | bytes 2048 | tf_op jit(solution)/shard_map/psum | solution.py:35
  421.3 1.3 multiply_divide_fusion
  422.6 0.0 copy-start.6
  422.6 2.1 multiply_convert_fusion
  424.7 0.3 copy-done.3
  425.0 0.6 copy-done.4
  425.6 2.9 subtract_bitcast_fusion
  (19 shorter events, 0.2 us)
Async XLA Ops:
  7.2 2.8 copy-start.7
  7.2 2.9 copy-start.1
  7.2 123.8 %all-reduce.6.cloned.1.call-start = ((), (), s32[]{:S(2)}) async-start(), calls=%async_computation | async-start | bytes 2097152 | tf_op jit(solution)/shard_map/psum | solution.py:30
  11.7 191.2 %all-reduce.8.cloned.1.call-start = ((), (), s32[]{:S(2)}) async-start(), calls=%async_computation.1 | async-start | bytes 524288 | tf_op jit(solution)/shard_map/psum | solution.py:31
  131.0 4.4 %copy-start.5 = (f32[1024,256]{1,0:T(8,128)S(1)}, f32[1024,256]{1,0:T(8,128)}, u32[]{:S(2)}) copy-start(f32[1024,256]{1,0:T(8,128)} %all-reduce.6.cloned.1.call-done) | copy-start | bytes 3145732
  135.2 191.1 %all-reduce.10.cloned.1.call-start = ((), (), s32[]{:S(2)}) async-start(), calls=%async_computation.2 | async-start | bytes 2097152 | tf_op jit(solution)/shard_map/psum | solution.py:34
  247.5 22.9 %copy-start = (bf16[1,1024,1024]{2,1,0:T(8,128)(2,1)S(1)}, bf16[1,1024,1024]{2,1,0:T(8,128)(2,1)}, u32[]{:S(2)}) copy-start(bf16[1,1024,1024]{2,1,0:T(8,128)(2,1)} %param.4) | copy-start | bytes 6291460
  269.7 1.6 copy-start.2
  273.3 129.7 %all-reduce.12.cloned.1.call-start = ((), (), s32[]{:S(2)}) async-start(), calls=%async_computation.3 | async-start | bytes 2097152 | tf_op jit(solution)/shard_map/psum | solution.py:34
  422.6 6.0 %copy-start.6 = (f32[1024,256]{1,0:T(8,128)}, f32[1024,256]{1,0:T(8,128)S(1)}, u32[]{:S(2)}) copy-start(f32[1024,256]{1,0:T(8,128)S(1)} %multiply_divide_fusion) | copy-start | bytes 3145732
  422.6 2.4 copy-start.3
  422.6 3.0 copy-start.4
Sparse Core Ops, SparseCore 0:
  11.9 119.1 all-reduce.5
  135.3 67.5 all-reduce.7
  273.4 52.9 all-reduce.9
  328.6 74.3 all-reduce.11
